TPU v7x, 256 devices: a whole 4x4x8 slice. The times are simulated.
256 devices in a mesh: seq: 32 (over y, z), ch: 8 (over x, core).
Axes of the slice: x: 4, y: 4, z: 8, core: 2. Of those that a mesh axis runs over, the one named last changes fastest.
Arguments:
- genome: int32 [8192, 128], P('seq'), may hold values from 0 to 3
- stem_weight: bfloat16 [768, 512], P('ch'), may hold values from -0.5 to 0.5
- dilated_filter_weight: bfloat16 [5, 3, 768, 768], P(None, None, 'ch'), may hold values from -0.125 to 0.125
- head_weight: bfloat16 [768, 5313], P('ch'), may hold values from -0.21875 to 0.21875
- window_start: int32 [512], replicated, may hold values from 0 to 8176
- window_track: int32 [512], replicated, may hold values from 0 to 5312
- targets: float32 [512], replicated, may hold values from 0 to 3
Outputs:
- window_score: float32 [512], replicated
- conv_grad: float32 [5, 3, 768, 768], P(None, None, 'ch', 'seq')
- stem_grad: float32 [768, 512], P('ch')
- head_grad: float32 [768, 5313], P('ch')
Inputs may be any that keep to these rules, and one draw needn't show every extreme that they name: `window_start`: each window lies inside the sequence.
All inputs are finite; a program needn't handle non-finite values.
Results may differ from a plain program's by a relative error of at most 0.0037.
Values may be sent and summed in bfloat16 or wider, within the bound.
A program may use at most 128 MiB of HBM per device.

v0:
```python
import jax
import jax.numpy as jnp
from jax import lax
from jax.sharding import PartitionSpec as P

LAYERS = 5
WIN = 16


def extended(block, sides, width):
    for axis, dim in sides:
        count = lax.axis_size(axis)
        forward = [(i, i + 1) for i in range(count - 1)]
        backward = [(target, source) for source, target in forward]
        low = lax.ppermute(
            lax.slice_in_dim(block, block.shape[dim] - width, None, axis=dim), axis, forward
        )
        high = lax.ppermute(lax.slice_in_dim(block, 0, width, axis=dim), axis, backward)
        block = jnp.concatenate([low, block, high], axis=dim)
    return block


def passed_along(value, axis, by):
    count = lax.axis_size(axis)
    pairs = [(i, i + by) for i in range(count) if 0 <= i + by < count]
    return lax.ppermute(value, axis, pairs)


def dilations(shard_rows):
    return (shard_rows // 8, shard_rows // 2, shard_rows, 2 * shard_rows, 4 * shard_rows)


def reach_rows(field, distance):
    shard_rows = field.shape[2]
    if distance < shard_rows:
        padded = extended(field, (("seq", 2),), distance)
        return (padded[:, :, :shard_rows], padded[:, :, 2 * distance :])
    hop_count = distance // shard_rows
    lower_rows = passed_along(field, "seq", hop_count)
    upper_rows = passed_along(field, "seq", -hop_count)
    return (lower_rows, upper_rows)


def order_taps(lower_rows, middle, upper_rows):
    forward_taps = jnp.stack([lower_rows[0], middle[0], upper_rows[0]])
    reverse_taps = jnp.stack([upper_rows[1], middle[1], lower_rows[1]])
    return jnp.stack([forward_taps, reverse_taps])


def shards(
    genome, stem_weight, dilated_filter_weight, head_weight, window_start, window_track, targets
):
    shard_rows = genome.shape[0]
    spans = dilations(shard_rows)
    letters = (
        (genome[:, :, None] == jnp.arange(4, dtype=jnp.int32))
        .astype(jnp.bfloat16)
        .reshape(shard_rows, -1)
    )
    strands = jnp.stack([letters, letters[:, ::-1]])
    residual_state = jnp.einsum(
        "sri,ci->scr", strands, stem_weight, preferred_element_type=jnp.float32
    )
    saved_states = []
    stored_taps = []
    for current_layer_index in range(LAYERS):
        active = jax.nn.gelu(residual_state).astype(jnp.bfloat16)
        lower_rows, upper_rows = reach_rows(active, spans[current_layer_index])
        resident_taps = order_taps(lower_rows, active, upper_rows)
        collected_taps = lax.all_gather(resident_taps, "ch", axis=2, tiled=True)
        saved_states.append(residual_state)
        stored_taps.append(collected_taps)
        residual_state = residual_state + jnp.einsum(
            "nezp,efz->nfp",
            collected_taps,
            dilated_filter_weight[current_layer_index],
            preferred_element_type=jnp.float32,
        )
    strand_total = residual_state[0] + residual_state[1]
    first_bin = lax.axis_index("seq") * shard_rows
    positions = first_bin + jnp.arange(shard_rows, dtype=jnp.int32)
    member = (
        (positions[None, :] >= window_start[:, None])
        & (positions[None, :] < window_start[:, None] + WIN)
    ).astype(jnp.float32)
    pooled = jnp.einsum("cr,kr->ck", strand_total, member, precision=lax.Precision.HIGHEST) / WIN
    columns = jnp.take(head_weight, window_track, axis=1).astype(jnp.float32)
    partial_score = 0.5 * jnp.sum(pooled * columns, axis=0)
    window_score = lax.psum(partial_score, ("seq", "ch"))
    counts = jnp.sum((window_track[:, None] == window_track[None, :]).astype(jnp.float32), axis=1)
    loss_slope = (jnp.exp(window_score) - targets) / counts
    window_terms = 0.5 * loss_slope[None, :] * pooled
    weights_back = 0.5 / WIN * loss_slope[None, :] * columns
    back_total = jnp.einsum("ck,kr->cr", weights_back, member, precision=lax.Precision.HIGHEST)
    grad_state = jnp.stack([back_total, back_total])
    layer_gradient_list = []
    for current_layer_index in reversed(range(LAYERS)):
        incoming_gradient = grad_state.astype(jnp.bfloat16)
        weight_part = jnp.einsum(
            "pygj,pij->yig",
            stored_taps[current_layer_index],
            incoming_gradient,
            preferred_element_type=jnp.float32,
        )
        layer_gradient_list.append(
            lax.psum_scatter(weight_part, "seq", scatter_dimension=2, tiled=True)
        )
        lower_rows, upper_rows = reach_rows(incoming_gradient, spans[current_layer_index])
        back_taps = order_taps(upper_rows, incoming_gradient, lower_rows)
        spread = jnp.einsum(
            "skor,koc->scr",
            back_taps,
            dilated_filter_weight[current_layer_index],
            preferred_element_type=jnp.float32,
        )
        through = lax.psum_scatter(spread, "ch", scatter_dimension=1, tiled=True)
        pullback = jax.vjp(jax.nn.gelu, saved_states[current_layer_index])[1]
        grad_state = grad_state + pullback(through)[0]
    conv_grad = jnp.stack(layer_gradient_list[::-1])
    stem_part = jnp.einsum(
        "sri,scr->ci", strands, grad_state.astype(jnp.bfloat16), preferred_element_type=jnp.float32
    )
    head_part = jnp.zeros(head_weight.shape, jnp.float32).at[:, window_track].add(window_terms)
    head_grad, stem_grad = lax.psum((head_part, stem_part), "seq")
    return (window_score, conv_grad, stem_grad, head_grad)


def solution(mesh):
    return jax.shard_map(
        shards,
        mesh=mesh,
        in_specs=(
            P("seq", None),
            P("ch", None),
            P(None, None, "ch", None),
            P("ch", None),
            P(),
            P(),
            P(),
        ),
        out_specs=(P(), P(None, None, "ch", "seq"), P("ch", None), P("ch", None)),
        check_vma=False,
    )
```

profile of v0, /device:TPU:1, one launch (start us, length us, event | category | flops | bytes accessed | tf_op | source)
XLA Modules:
  0.0 820.2 jit_solution(104383886669573757)
XLA Ops:
  10.7 4.5 collective-permute-start
  15.2 1.3 collective-permute-start.1
  16.5 3.7 collective-permute-done.1
  21.2 32.7 %all-gather.6.cloned.1.call-done = bf16[2,3,768,256]{3,2,1,0:T(8,128)(2,1)} async-done(((bf16[2,3,96,256]{3,2,1,0:T(8,128)(2,1)}), bf16[2,3,768,256]{3,2,1,0:T(8,128)(2,1)}) %all-gather.6.cloned.1.call-update) | async-done | bytes 2359312 | tf_op jit(solution)/shard_map/all_gather | solution.py:70
  53.9 2.2 multiply_convert_fusion.3
  56.1 3.2 collective-permute-start.2
  59.3 1.3 collective-permute-start.3
  60.7 3.5 collective-permute-done.3
  65.0 30.5 %all-gather.8.cloned.1.call-done = bf16[2,3,768,256]{3,2,1,0:T(8,128)(2,1)} async-done(((bf16[2,3,96,256]{3,2,1,0:T(8,128)(2,1)}), bf16[2,3,768,256]{3,2,1,0:T(8,128)(2,1)}) %all-gather.8.cloned.1.call-update) | async-done | bytes 2359312 | tf_op jit(solution)/shard_map/all_gather | solution.py:70
  95.5 2.2 multiply_convert_fusion.2
  97.7 3.2 collective-permute-start.4
  100.9 1.3 collective-permute-start.5
  102.8 3.8 collective-permute-done.5
  107.5 30.2 %all-gather.10.cloned.1.call-done = bf16[2,3,768,256]{3,2,1,0:T(8,128)(2,1)} async-done(((bf16[2,3,96,256]{3,2,1,0:T(8,128)(2,1)}), bf16[2,3,768,256]{3,2,1,0:T(8,128)(2,1)}) %all-gather.10.cloned.1.call-update) | async-done | bytes 2359312 | tf_op jit(solution)/shard_map/all_gather | solution.py:70
  137.6 2.2 multiply_convert_fusion.1
  139.9 4.2 collective-permute-start.6
  144.0 1.3 collective-permute-start.7
  145.9 8.8 %collective-permute-done.7 = bf16[2,96,256]{2,1,0:T(8,128)(2,1)S(1)} collective-permute-done((bf16[2,96,256]{2,1,0:T(8,128)(2,1)S(1)}, bf16[2,96,256]{2,1,0:T(8,128)(2,1)S(1)}, u32[]{:S(2)}, u32[]{:S(2)}) %collective-permute-start.7) | collective-permute-done | bytes 98336 | tf_op jit(solution)/shard_map/ppermute | solution.py:26
  155.6 27.2 %all-gather.12.cloned.1.call-done = bf16[2,3,768,256]{3,2,1,0:T(8,128)(2,1)} async-done(((bf16[2,3,96,256]{3,2,1,0:T(8,128)(2,1)}), bf16[2,3,768,256]{3,2,1,0:T(8,128)(2,1)}) %all-gather.12.cloned.1.call-update) | async-done | bytes 2359312 | tf_op jit(solution)/shard_map/all_gather | solution.py:70
  182.8 2.2 multiply_convert_fusion
  185.0 7.4 collective-permute-start.8
  192.4 1.3 collective-permute-start.9
  194.2 8.6 %collective-permute-done.9 = bf16[2,96,256]{2,1,0:T(8,128)(2,1)S(1)} collective-permute-done((bf16[2,96,256]{2,1,0:T(8,128)(2,1)S(1)}, bf16[2,96,256]{2,1,0:T(8,128)(2,1)S(1)}, u32[]{:S(2)}, u32[]{:S(2)}) %collective-permute-start.9) | collective-permute-done | bytes 98336 | tf_op jit(solution)/shard_map/ppermute | solution.py:26
  203.6 2.4 copy.74
  206.1 2.6 gather_fusion
  209.1 22.5 %all-gather.14.cloned.1.call-done = bf16[2,3,768,256]{3,2,1,0:T(8,128)(2,1)} async-done(((bf16[2,3,96,256]{3,2,1,0:T(8,128)(2,1)}), bf16[2,3,768,256]{3,2,1,0:T(8,128)(2,1)}) %all-gather.14.cloned.1.call-update) | async-done | bytes 2359312 | tf_op jit(solution)/shard_map/all_gather | solution.py:70
  231.6 2.2 fusion.6
  233.8 1.2 fusion.102
  235.0 76.7 %psum.21 = f32[512]{0:T(512)S(1)} all-reduce(f32[512]{0:T(512)S(1)} %broadcast_multiply_fusion), channel_id=1, replica_groups=mesh['seq'=32,'ch'=8] {'seq','ch'}, use_global_device_ids=true, to_apply=%region_1.2 | all-reduce | flops 512 | bytes 4096 | tf_op jit(solution)/shard_map/psum | solution.py:89
  312.2 1.3 collective-permute-start.10
  313.5 7.9 collective-permute-start.11
  321.6 4.9 collective-permute-done.11
  326.5 1.8 convolution_bitcast_fusion.4
  328.3 32.8 %reduce-scatter.6.cloned.1.call-done = f32[2,96,256]{2,1,0:T(8,128)} async-done(((f32[2,768,256]{2,1,0:T(8,128)}), f32[2,96,256]{2,1,0:T(8,128)}) %reduce-scatter.6.cloned.1.call-update) | async-done | bytes 196624 | tf_op jit(solution)/shard_map/reduce_scatter | solution.py:116
  362.3 1.3 collective-permute-start.12
  363.6 4.9 collective-permute-start.13
  370.1 1.8 convolution_bitcast_fusion.3
  372.0 39.8 %reduce-scatter.8.cloned.1.call-done = f32[2,96,256]{2,1,0:T(8,128)} async-done(((f32[2,768,256]{2,1,0:T(8,128)}), f32[2,96,256]{2,1,0:T(8,128)}) %reduce-scatter.8.cloned.1.call-update) | async-done | bytes 196624 | tf_op jit(solution)/shard_map/reduce_scatter | solution.py:116
  412.9 1.3 collective-permute-start.14
  414.2 4.0 collective-permute-start.15
  418.3 1.5 collective-permute-done.15
  419.9 1.8 convolution_bitcast_fusion.2
  421.7 37.6 %reduce-scatter.10.cloned.1.call-done = f32[2,96,256]{2,1,0:T(8,128)} async-done(((f32[2,768,256]{2,1,0:T(8,128)}), f32[2,96,256]{2,1,0:T(8,128)}) %reduce-scatter.10.cloned.1.call-update) | async-done | bytes 196624 | tf_op jit(solution)/shard_map/reduce_scatter | solution.py:116
  460.4 1.3 collective-permute-start.16
  461.7 4.0 collective-permute-start.17
  465.7 1.1 collective-permute-done.17
  466.9 1.8 convolution_bitcast_fusion.1
  468.7 37.7 %reduce-scatter.12.cloned.1.call-done = f32[2,96,256]{2,1,0:T(8,128)} async-done(((f32[2,768,256]{2,1,0:T(8,128)}), f32[2,96,256]{2,1,0:T(8,128)}) %reduce-scatter.12.cloned.1.call-update) | async-done | bytes 196624 | tf_op jit(solution)/shard_map/reduce_scatter | solution.py:116
  506.4 1.8 fusion.169
  508.2 1.3 collective-permute-start.18
  509.5 4.2 collective-permute-start.19
  514.8 2.9 convolution_bitcast_fusion
  519.6 1.6 copy.89
  521.2 4.4 scatter_custom_fusion
  525.5 2.6 convolution_bitcast_fusion.6
  528.2 1.5 copy.87
  530.6 1.5 copy.85
  532.1 2.7 convolution_bitcast_fusion.8
  534.8 1.5 copy.83
  537.2 1.5 copy.81
  538.7 16.7 %reduce-scatter.14.cloned.1.call-done = f32[2,96,256]{2,1,0:T(8,128)} async-done(((f32[2,768,256]{2,1,0:T(8,128)}), f32[2,96,256]{2,1,0:T(8,128)}) %reduce-scatter.14.cloned.1.call-update) | async-done | bytes 196624 | tf_op jit(solution)/shard_map/reduce_scatter | solution.py:116
  555.5 1.9 convolution_bitcast_fusion.15
  559.3 246.3 %all-reduce.8.cloned.1.call-done = (f32[3,96,768]{1,0,2:T(4,128)}, f32[3,96,768]{1,0,2:T(4,128)}, f32[3,96,768]{1,0,2:T(4,128)}, f32[3,96,768]{1,0,2:T(4,128)}, ...) async-done(((f32[3,96,768]{1,0,2:T(4,128)}, f32[3,96,768]{1,0,2:T(4,128)}, f32[3,96,768]{1,0,2:T(4,128)}, f32[3,96,768]{1,0,2:T(4,128)}, ...) | async-done | bytes 6660496
  805.6 3.2 copy.97
  (173 shorter events, 26.3 us)
Async XLA Ops:
  7.2 3.1 copy-start
  7.2 46.7 %all-gather.6.cloned.1.call-start = ((), (), s32[]{:S(2)}) async-start(), calls=%async_computation.5 | async-start | bytes 2654208 | tf_op jit(solution)/shard_map/all_gather | solution.py:70
  9.9 11.2 %copy-start.12 = (bf16[256,512]{1,0:T(8,128)(2,1)}, bf16[256,512]{1,0:T(8,128)(2,1)S(1)}, u32[]{:S(2)}) copy-start(bf16[256,512]{1,0:T(8,128)(2,1)S(1)} %rev.3) | copy-start | bytes 786436
  10.2 43.7 %copy-start.5 = (bf16[5,3,96,768]{3,2,1,0:T(8,128)(2,1)S(1)}, bf16[5,3,96,768]{3,2,1,0:T(8,128)(2,1)}, u32[]{:S(2)}) copy-start(bf16[5,3,96,768]{3,2,1,0:T(8,128)(2,1)} %param.9) | copy-start | bytes 6635524
  10.2 10.0 %copy-start.10 = (bf16[1,256,512]{2,1,0:T(8,128)(2,1)}, bf16[1,256,512]{2,1,0:T(8,128)(2,1)S(1)}, u32[]{:S(2)}) copy-start(bf16[1,256,512]{2,1,0:T(8,128)(2,1)S(1)} %compare_convert_fusion.1) | copy-start | bytes 786436
  10.6 45.5 %copy-start.14 = (f32[2,96,256]{2,1,0:T(8,128)}, f32[2,96,256]{2,1,0:T(8,128)S(1)}, u32[]{:S(2)}) copy-start(f32[2,96,256]{2,1,0:T(8,128)S(1)} %get-tuple-element.96) | copy-start | bytes 589828
  10.7 5.8 collective-permute-start
  15.2 5.0 collective-permute-start.1
  21.1 74.3 %all-gather.8.cloned.1.call-start = ((), (), s32[]{:S(2)}) async-start(), calls=%async_computation.6 | async-start | bytes 2654208 | tf_op jit(solution)/shard_map/all_gather | solution.py:70
  56.1 4.5 collective-permute-start.2
  59.3 4.8 collective-permute-start.3
  65.0 72.7 %all-gather.10.cloned.1.call-start = ((), (), s32[]{:S(2)}) async-start(), calls=%async_computation.7 | async-start | bytes 2654208 | tf_op jit(solution)/shard_map/all_gather | solution.py:70
  97.7 5.0 collective-permute-start.4
  100.9 5.7 collective-permute-start.5
  107.4 75.4 %all-gather.12.cloned.1.call-start = ((), (), s32[]{:S(2)}) async-start(), calls=%async_computation.8 | async-start | bytes 2654208 | tf_op jit(solution)/shard_map/all_gather | solution.py:70
  139.9 6.0 collective-permute-start.6
  144.0 10.6 %collective-permute-start.7 = (bf16[2,96,256]{2,1,0:T(8,128)(2,1)S(1)}, bf16[2,96,256]{2,1,0:T(8,128)(2,1)S(1)}, u32[]{:S(2)}, u32[]{:S(2)}) collective-permute-start(bf16[2,96,256]{2,1,0:T(8,128)(2,1)S(1)} %get-tuple-element.101), channel_id=1, source_target_pairs={{16,0},{24,8},{32,16},{40,24},{48,32},{56,40},{64,48},{72,56},{80,... | collective-permute-start | bytes 294920 | tf_op jit(solution)/shard_map/ppermute | solution.py:26
  155.5 76.1 %all-gather.14.cloned.1.call-start = ((), (), s32[]{:S(2)}) async-start(), calls=%async_computation.9 | async-start | bytes 2654208 | tf_op jit(solution)/shard_map/all_gather | solution.py:70
  185.0 21.1 %copy-start.19 = (s32[512]{0:T(512)S(1)}, s32[512]{0:T(512)}, u32[]{:S(2)}) copy-start(s32[512]{0:T(512)} %param.12) | copy-start | bytes 6148
  185.0 9.1 %collective-permute-start.8 = (bf16[2,96,256]{2,1,0:T(8,128)(2,1)S(1)}, bf16[2,96,256]{2,1,0:T(8,128)(2,1)S(1)}, u32[]{:S(2)}, u32[]{:S(2)}) collective-permute-start(bf16[2,96,256]{2,1,0:T(8,128)(2,1)S(1)} %get-tuple-element.103), channel_id=1, source_target_pairs={{0,32},{8,40},{16,48},{24,56},{32,64},{40,72},{48,80},{56,88},{64,... | collective-permute-start | bytes 294920 | tf_op jit(solution)/shard_map/ppermute | solution.py:26
  192.4 10.3 %collective-permute-start.9 = (bf16[2,96,256]{2,1,0:T(8,128)(2,1)S(1)}, bf16[2,96,256]{2,1,0:T(8,128)(2,1)S(1)}, u32[]{:S(2)}, u32[]{:S(2)}) collective-permute-start(bf16[2,96,256]{2,1,0:T(8,128)(2,1)S(1)} %get-tuple-element.103), channel_id=1, source_target_pairs={{32,0},{40,8},{48,16},{56,24},{64,32},{72,40},{80,48},{88,56},{96,... | collective-permute-start | bytes 294920 | tf_op jit(solution)/shard_map/ppermute | solution.py:26
  202.8 6.3 copy-start.22
  203.6 157.6 %reduce-scatter.6.cloned.1.call-start = ((), (), s32[]{:S(2)}) async-start(), calls=%async_computation.10 | async-start | bytes 1769472 | tf_op jit(solution)/shard_map/reduce_scatter | solution.py:116
  208.7 103.0 %copy-start.23 = (f32[512]{0:T(512)S(1)}, f32[512]{0:T(512)}, u32[]{:S(2)}) copy-start(f32[512]{0:T(512)} %param.13) | copy-start | bytes 6148
  311.7 16.6 %copy-start.20 = (f32[512]{0:T(512)}, f32[512]{0:T(512)S(1)}, u32[]{:S(2)}) copy-start(f32[512]{0:T(512)S(1)} %psum.21) | copy-start | bytes 6148
  312.2 9.4 %collective-permute-start.10 = (bf16[2,96,256]{2,1,0:T(8,128)(2,1)S(1)}, bf16[2,96,256]{2,1,0:T(8,128)(2,1)S(1)}, u32[]{:S(2)}, u32[]{:S(2)}) collective-permute-start(bf16[2,96,256]{2,1,0:T(8,128)(2,1)S(1)} %fusion.101), channel_id=1, source_target_pairs={{32,0},{40,8},{48,16},{56,24},{64,32},{72,40},{80,48},{88,56},{96,... | collective-permute-start | bytes 294920 | tf_op jit(solution)/shard_map/ppermute | solution.py:26
  313.5 13.0 %collective-permute-start.11 = (bf16[2,96,256]{2,1,0:T(8,128)(2,1)S(1)}, bf16[2,96,256]{2,1,0:T(8,128)(2,1)S(1)}, u32[]{:S(2)}, u32[]{:S(2)}) collective-permute-start(bf16[2,96,256]{2,1,0:T(8,128)(2,1)S(1)} %fusion.101), channel_id=1, source_target_pairs={{0,32},{8,40},{16,48},{24,56},{32,64},{40,72},{48,80},{56,88},{64,... | collective-permute-start | bytes 294920 | tf_op jit(solution)/shard_map/ppermute | solution.py:26
  328.3 83.5 %reduce-scatter.8.cloned.1.call-start = ((), (), s32[]{:S(2)}) async-start(), calls=%async_computation.11 | async-start | bytes 1769472 | tf_op jit(solution)/shard_map/reduce_scatter | solution.py:116
  362.3 9.7 %copy-start.6 = (bf16[2,96,256]{2,1,0:T(8,128)(2,1)}, bf16[2,96,256]{2,1,0:T(8,128)(2,1)S(1)}, u32[]{:S(2)}) copy-start(bf16[2,96,256]{2,1,0:T(8,128)(2,1)S(1)} %get-tuple-element.33) | copy-start | bytes 294916
  362.3 7.3 collective-permute-start.12
  363.6 6.5 collective-permute-start.13
  371.9 87.4 %reduce-scatter.10.cloned.1.call-start = ((), (), s32[]{:S(2)}) async-start(), calls=%async_computation.12 | async-start | bytes 1769472 | tf_op jit(solution)/shard_map/reduce_scatter | solution.py:116
  412.9 8.8 %copy-start.8 = (bf16[2,96,256]{2,1,0:T(8,128)(2,1)}, bf16[2,96,256]{2,1,0:T(8,128)(2,1)S(1)}, u32[]{:S(2)}) copy-start(bf16[2,96,256]{2,1,0:T(8,128)(2,1)S(1)} %get-tuple-element.31) | copy-start | bytes 294916
  412.9 5.4 collective-permute-start.14
  414.2 5.6 collective-permute-start.15
  421.7 84.7 %reduce-scatter.12.cloned.1.call-start = ((), (), s32[]{:S(2)}) async-start(), calls=%async_computation.13 | async-start | bytes 1769472 | tf_op jit(solution)/shard_map/reduce_scatter | solution.py:116
  460.4 5.3 collective-permute-start.16
  461.7 5.2 collective-permute-start.17
  468.7 86.8 %reduce-scatter.14.cloned.1.call-start = ((), (), s32[]{:S(2)}) async-start(), calls=%async_computation.14 | async-start | bytes 1769472 | tf_op jit(solution)/shard_map/reduce_scatter | solution.py:116
  508.2 5.5 collective-permute-start.18
  509.5 5.2 collective-permute-start.19
  514.7 3.1 copy-start.17
  514.8 3.9 copy-start.4
  517.8 287.8 %all-reduce.8.cloned.1.call-start = ((), (), s32[]{:S(2)}) async-start(), calls=%async_computation.15 | async-start | bytes 21569536
  519.5 6.0 copy-start.7
  525.5 4.2 copy-start.3
  528.2 1.6 copy-start.9
  532.1 4.3 copy-start.2
  537.2 18.3 %copy-start.11 = (bf16[1,256,512]{2,1,0:T(8,128)(2,1)S(1)}, bf16[1,256,512]{2,1,0:T(8,128)(2,1)}, u32[]{:S(2)}) copy-start(bf16[1,256,512]{2,1,0:T(8,128)(2,1)} %copy-done.10) | copy-start | bytes 786436
  537.2 18.3 %copy-start.13 = (bf16[256,512]{1,0:T(8,128)(2,1)S(1)}, bf16[256,512]{1,0:T(8,128)(2,1)}, u32[]{:S(2)}) copy-start(bf16[256,512]{1,0:T(8,128)(2,1)} %copy-done.12) | copy-start | bytes 786436
  537.2 18.3 %copy-start.15 = (f32[2,96,256]{2,1,0:T(8,128)S(1)}, f32[2,96,256]{2,1,0:T(8,128)}, u32[]{:S(2)}) copy-start(f32[2,96,256]{2,1,0:T(8,128)} %copy-done.14) | copy-start | bytes 589828
  537.2 18.2 %copy-start.16 = (f32[2,96,256]{2,1,0:T(8,128)S(1)}, f32[2,96,256]{2,1,0:T(8,128)}, u32[]{:S(2)}) copy-start(f32[2,96,256]{2,1,0:T(8,128)} %get-tuple-element.28) | copy-start | bytes 589828
  557.4 0.7 copy-start.24
  805.6 8.1 copy-start.1
  805.6 7.4 copy-start.18
  813.0 0.7 copy-start.21
Sparse Core Ops, SparseCore 0:
  21.3 32.5 all-gather.5
  65.1 30.3 all-gather.7
  107.5 30.0 all-gather.9
  155.6 27.1 all-gather.11
  203.7 27.8 all-gather.13
  328.4 32.7 reduce-scatter.5
  372.0 39.7 reduce-scatter.7
  421.8 37.4 reduce-scatter.9
  468.8 37.5 reduce-scatter.11
  517.9 37.4 reduce-scatter.13
  560.7 244.8 all-reduce.7
where the time goes:
time: 822 us; the launch traced here: 820 us
  waiting for transfers between devices  594 us (72%)
  blocking collectives  76.7 us (9%)
  starting transfers between devices  60.7 us (7%)
  matrix products  32.7 us (4%)
  local copies, waits for them, and re-layouts  26.2 us (3%)
  between operations  15.4 us (2%)
  other arithmetic  14 us (2%)
    unnamed x12, waiting for transfers between devices  247 us
    reduce_scatter x5, waiting for transfers between devices, shards(): through = lax.psum_scatter(spread, 'ch', scatter_dimension=1, tiled=True)  165 us
    all_gather x5, waiting for transfers between devices, shards(): collected_taps = lax.all_gather(resident_taps, 'ch', axis=2, tiled=True)  143 us
    psum x1, blocking collectives, shards(): window_score = lax.psum(partial_score, ('seq', 'ch'))  76.7 us
    ppermute x12, starting transfers between devices, passed_along(): return lax.ppermute(value, axis, pairs)  39.3 us
    ppermute x12, waiting for transfers between devices, passed_along(): return lax.ppermute(value, axis, pairs)  30.9 us
  transfers between devices with their start and end apart: 31, of which 26 were waited for; matrix products, arithmetic and copies ran while one was open for 3% of the time, Pallas kernels for 0%

commit v1 on v0

--- a/solution.py
+++ b/solution.py
@@ -5,6 +5,17 @@
 
 LAYERS = 5
 WIN = 16
+
+
+def pass_along(x, axis, d):
+    size = lax.axis_size(axis)
+    right = [(i, (i + 1) % size) for i in range(size)]
+    pieces = [x]
+    for hop in range(1, size):
+        pieces = [lax.ppermute(pieces[0], axis, right), *pieces]
+    whole = jnp.concatenate(pieces, axis=d)
+    shift = (lax.axis_index(axis) + 1) * pieces[-1].shape[d]
+    return jnp.roll(whole, shift, axis=d)
 
 
 def extended(block, sides, width):
@@ -67,7 +78,7 @@
         active = jax.nn.gelu(residual_state).astype(jnp.bfloat16)
         lower_rows, upper_rows = reach_rows(active, spans[current_layer_index])
         resident_taps = order_taps(lower_rows, active, upper_rows)
-        collected_taps = lax.all_gather(resident_taps, "ch", axis=2, tiled=True)
+        collected_taps = pass_along(resident_taps, "ch", 2)
         saved_states.append(residual_state)
         stored_taps.append(collected_taps)
         residual_state = residual_state + jnp.einsum(

time: 822 us -> 934 us (1.14)
  waiting for transfers between devices: 594 us -> 675 us
  starting transfers between devices: 60.7 us -> 80.6 us
  matrix products: 32.7 us -> 42.3 us
    ppermute x0 -> x35, waiting for transfers between devices: none -> 241 us  [pass_along(): pieces = [lax.ppermute(pieces[0], axis, right), *pieces]]
    all_gather x5 -> x0, waiting for transfers between devices: 143 us -> none  [shards(): collected_taps = lax.all_gather(resident_taps, 'ch', axis=2, tiled=True)]
    ppermute x0 -> x35, starting transfers between devices: none -> 15 us  [pass_along(): pieces = [lax.ppermute(pieces[0], axis, right), *pieces]]
    dot_general x5, matrix products: 7.84 us -> 18.3 us  [shards(): jnp.einsum('pygj,pij->yig', stored_taps[current_layer_index], incoming_gr...]
    unnamed x12 -> x7, waiting for transfers between devices: 247 us -> 246 us
  transfers between devices with their start and end apart: 31 -> 61, of which waited for: 26 -> 56; matrix products, arithmetic and copies ran while one was open for 3% -> 4% of each run, Pallas kernels for 0% -> 0%
where the time goes in v1:
time: 934 us; the launch traced here: 932 us
  waiting for transfers between devices  675 us (72%)
  blocking collectives  82.8 us (9%)
  starting transfers between devices  80.6 us (9%)
  matrix products  42.3 us (5%)
  local copies, waits for them, and re-layouts  25.7 us (3%)
  between operations  16.3 us (2%)
  other arithmetic  9.43 us (1%)
    unnamed x7, waiting for transfers between devices  246 us
    ppermute x35, waiting for transfers between devices, pass_along(): pieces = [lax.ppermute(pieces[0], axis, right), *pieces]  241 us
    reduce_scatter x5, waiting for transfers between devices, shards(): through = lax.psum_scatter(spread, 'ch', scatter_dimension=1, tiled=True)  158 us
    psum x1, blocking collectives, shards(): window_score = lax.psum(partial_score, ('seq', 'ch'))  82.8 us
    ppermute x12, starting transfers between devices, passed_along(): return lax.ppermute(value, axis, pairs)  43.2 us
    ppermute x12, waiting for transfers between devices, passed_along(): return lax.ppermute(value, axis, pairs)  23 us
  transfers between devices with their start and end apart: 61, of which 56 were waited for; matrix products, arithmetic and copies ran while one was open for 4% of the time, Pallas kernels for 0%

profile of v1, /device:TPU:1, one launch (start us, length us, event | category | flops | bytes accessed | tf_op | source)
XLA Modules:
  0.0 932.2 jit_solution(16346334550598194519)
XLA Ops:
  10.7 4.4 collective-permute-start
  16.4 3.7 collective-permute-done.1
  20.3 3.0 collective-permute-start.2
  23.3 3.7 collective-permute-done.2
  29.5 3.7 collective-permute-done.3
  35.6 3.7 collective-permute-done.4
  41.8 3.7 collective-permute-done.5
  47.9 4.8 collective-permute-done.6
  54.1 6.0 collective-permute-done.7
  60.2 7.2 collective-permute-done.8
  71.2 4.2 collective-permute-start.9
  76.6 8.3 collective-permute-done.11
  84.9 7.4 collective-permute-done.12
  92.3 7.4 collective-permute-done.13
  99.6 7.4 collective-permute-done.14
  107.0 7.4 collective-permute-done.15
  114.4 7.4 collective-permute-done.16
  121.7 7.4 collective-permute-done.17
  131.5 4.6 collective-permute-start.18
  137.7 5.2 collective-permute-done.19
  143.0 8.5 collective-permute-done.20
  151.5 7.4 collective-permute-done.21
  158.9 7.4 collective-permute-done.22
  166.2 7.4 collective-permute-done.23
  173.6 7.4 collective-permute-done.24
  181.0 7.4 collective-permute-done.25
  188.3 7.4 collective-permute-done.26
  198.1 7.8 collective-permute-start.27
  207.6 4.6 collective-permute-done.28
  212.5 8.6 collective-permute-done.29
  221.1 7.4 collective-permute-done.30
  228.5 7.4 collective-permute-done.31
  235.8 7.4 collective-permute-done.32
  243.2 7.4 collective-permute-done.33
  250.5 7.4 collective-permute-done.34
  257.9 7.4 collective-permute-done.35
  268.3 6.1 collective-permute-start.36
  276.0 7.6 collective-permute-done.37
  284.0 8.6 collective-permute-done.38
  292.6 7.4 collective-permute-done.39
  300.0 7.4 collective-permute-done.40
  308.5 6.2 collective-permute-done.41
  316.2 6.0 collective-permute-done.42
  322.4 7.3 collective-permute-done.43
  329.8 7.3 collective-permute-done.44
  342.6 82.8 %psum.21 = f32[512]{0:T(512)S(1)} all-reduce(f32[512]{0:T(512)S(1)} %broadcast_multiply_fusion), channel_id=1, replica_groups=mesh['seq'=32,'ch'=8] {'seq','ch'}, use_global_device_ids=true, to_apply=%region_1.3 | all-reduce | flops 512 | bytes 4096 | tf_op jit(solution)/shard_map/psum | solution.py:100
  427.2 7.9 collective-permute-start.46
  438.6 36.0 %reduce-scatter.6.cloned.1.call-done = f32[2,96,256]{2,1,0:T(8,128)} async-done(((f32[2,768,256]{2,1,0:T(8,128)}), f32[2,96,256]{2,1,0:T(8,128)}) %reduce-scatter.6.cloned.1.call-update) | async-done | bytes 196624 | tf_op jit(solution)/shard_map/reduce_scatter | solution.py:127
  477.0 4.9 collective-permute-start.48
  485.4 39.8 %reduce-scatter.8.cloned.1.call-done = f32[2,96,256]{2,1,0:T(8,128)} async-done(((f32[2,768,256]{2,1,0:T(8,128)}), f32[2,96,256]{2,1,0:T(8,128)}) %reduce-scatter.8.cloned.1.call-update) | async-done | bytes 196624 | tf_op jit(solution)/shard_map/reduce_scatter | solution.py:127
  527.5 4.0 collective-permute-start.50
  535.0 37.7 %reduce-scatter.10.cloned.1.call-done = f32[2,96,256]{2,1,0:T(8,128)} async-done(((f32[2,768,256]{2,1,0:T(8,128)}), f32[2,96,256]{2,1,0:T(8,128)}) %reduce-scatter.10.cloned.1.call-update) | async-done | bytes 196624 | tf_op jit(solution)/shard_map/reduce_scatter | solution.py:127
  575.3 4.0 collective-permute-start.52
  582.3 37.6 %reduce-scatter.12.cloned.1.call-done = f32[2,96,256]{2,1,0:T(8,128)} async-done(((f32[2,768,256]{2,1,0:T(8,128)}), f32[2,96,256]{2,1,0:T(8,128)}) %reduce-scatter.12.cloned.1.call-update) | async-done | bytes 196624 | tf_op jit(solution)/shard_map/reduce_scatter | solution.py:127
  622.5 4.2 collective-permute-start.54
  629.8 3.7 convolution_bitcast_fusion.5
  635.0 3.9 scatter_custom_fusion
  638.9 3.6 convolution_bitcast_fusion.6
  644.1 3.7 convolution_bitcast_fusion.7
  649.4 3.7 convolution_bitcast_fusion.8
  654.7 3.7 convolution_bitcast_fusion.9
  659.9 7.4 reduce-scatter.14.cloned.1.call-done
  671.1 246.1 %all-reduce.8.cloned.1.call-done = (f32[3,96,768]{1,0,2:T(4,128)}, f32[3,96,768]{1,0,2:T(4,128)}, f32[3,96,768]{1,0,2:T(4,128)}, f32[3,96,768]{1,0,2:T(4,128)}, ...) async-done(((f32[3,96,768]{1,0,2:T(4,128)}, f32[3,96,768]{1,0,2:T(4,128)}, f32[3,96,768]{1,0,2:T(4,128)}, f32[3,96,768]{1,0,2:T(4,128)}, ...) | async-done | bytes 6660496
  917.2 3.2 copy.97
  (296 shorter events, 86.3 us)
Async XLA Ops:
  7.2 467.4 %reduce-scatter.6.cloned.1.call-start = ((), (), s32[]{:S(2)}) async-start(), calls=%async_computation.5 | async-start | bytes 1769472 | tf_op jit(solution)/shard_map/reduce_scatter | solution.py:127
  10.7 5.7 collective-permute-start
  15.1 5.0 collective-permute-start.1
  20.3 6.7 collective-permute-start.2
  27.0 6.1 collective-permute-start.3
  33.1 6.1 collective-permute-start.4
  39.3 6.1 collective-permute-start.5
  45.4 7.3 collective-permute-start.6
  52.7 7.4 collective-permute-start.7
  60.1 7.4 collective-permute-start.8
  69.9 5.5 collective-permute-start.10
  71.2 5.3 collective-permute-start.9
  76.6 8.3 collective-permute-start.11
  84.9 7.4 collective-permute-start.12
  92.3 7.4 collective-permute-start.13
  99.6 7.4 collective-permute-start.14
  107.0 7.4 collective-permute-start.15
  114.4 7.4 collective-permute-start.16
  121.7 7.4 collective-permute-start.17
  131.5 64.4 %copy-start.18 = (f32[2,96,256]{2,1,0:T(8,128)}, f32[2,96,256]{2,1,0:T(8,128)S(1)}, u32[]{:S(2)}) copy-start(f32[2,96,256]{2,1,0:T(8,128)S(1)} %get-tuple-element.101) | copy-start | bytes 589828
  131.5 6.2 collective-permute-start.18
  136.1 6.8 collective-permute-start.19
  143.0 8.5 collective-permute-start.20
  151.5 7.4 collective-permute-start.21
  158.9 7.4 collective-permute-start.22
  166.2 7.4 collective-permute-start.23
  173.6 7.4 collective-permute-start.24
  181.0 7.4 collective-permute-start.25
  188.3 7.4 collective-permute-start.26
  198.1 67.4 %copy-start.20 = (f32[2,96,256]{2,1,0:T(8,128)}, f32[2,96,256]{2,1,0:T(8,128)S(1)}, u32[]{:S(2)}) copy-start(f32[2,96,256]{2,1,0:T(8,128)S(1)} %get-tuple-element.103) | copy-start | bytes 589828
  198.1 9.5 %collective-permute-start.27 = (bf16[2,96,256]{2,1,0:T(8,128)(2,1)S(1)}, bf16[2,96,256]{2,1,0:T(8,128)(2,1)S(1)}, u32[]{:S(2)}, u32[]{:S(2)}) collective-permute-start(bf16[2,96,256]{2,1,0:T(8,128)(2,1)S(1)} %get-tuple-element.102), channel_id=1, source_target_pairs={{0,16},{8,24},{16,32},{24,40},{32,48},{40,56},{48,64},{56,72},{64,... | collective-permute-start | bytes 294920 | tf_op jit(solution)/shard_map/ppermute | solution.py:37
  205.9 6.3 collective-permute-start.28
  212.3 8.8 collective-permute-start.29
  221.1 7.4 collective-permute-start.30
  228.5 7.4 collective-permute-start.31
  235.8 7.4 collective-permute-start.32
  243.2 7.4 collective-permute-start.33
  250.5 7.4 collective-permute-start.34
  257.9 7.4 collective-permute-start.35
  268.3 7.7 collective-permute-start.36
  274.4 9.3 collective-permute-start.37
  283.8 8.8 collective-permute-start.38
  292.6 7.4 collective-permute-start.39
  300.0 7.4 collective-permute-start.40
  307.3 7.4 collective-permute-start.41
  314.7 7.5 collective-permute-start.42
  322.2 7.5 collective-permute-start.43
  329.7 7.4 collective-permute-start.44
  339.3 86.2 %copy-start.35 = (f32[512]{0:T(512)S(1)}, f32[512]{0:T(512)}, u32[]{:S(2)}) copy-start(f32[512]{0:T(512)} %param.15) | copy-start | bytes 6148
  425.9 9.3 %collective-permute-start.45 = (bf16[2,96,256]{2,1,0:T(8,128)(2,1)S(1)}, bf16[2,96,256]{2,1,0:T(8,128)(2,1)S(1)}, u32[]{:S(2)}, u32[]{:S(2)}) collective-permute-start(bf16[2,96,256]{2,1,0:T(8,128)(2,1)S(1)} %fusion.106), channel_id=1, source_target_pairs={{32,0},{40,8},{48,16},{56,24},{64,32},{72,40},{80,48},{88,56},{96,... | collective-permute-start | bytes 294920 | tf_op jit(solution)/shard_map/ppermute | solution.py:37
  427.2 9.5 %collective-permute-start.46 = (bf16[2,96,256]{2,1,0:T(8,128)(2,1)S(1)}, bf16[2,96,256]{2,1,0:T(8,128)(2,1)S(1)}, u32[]{:S(2)}, u32[]{:S(2)}) collective-permute-start(bf16[2,96,256]{2,1,0:T(8,128)(2,1)S(1)} %fusion.106), channel_id=1, source_target_pairs={{0,32},{8,40},{16,48},{24,56},{32,64},{40,72},{48,80},{56,88},{64,... | collective-permute-start | bytes 294920 | tf_op jit(solution)/shard_map/ppermute | solution.py:37
  438.6 86.6 %reduce-scatter.8.cloned.1.call-start = ((), (), s32[]{:S(2)}) async-start(), calls=%async_computation.6 | async-start | bytes 1769472 | tf_op jit(solution)/shard_map/reduce_scatter | solution.py:127
  475.7 7.3 collective-permute-start.47
  477.0 6.5 collective-permute-start.48
  485.3 87.4 %reduce-scatter.10.cloned.1.call-start = ((), (), s32[]{:S(2)}) async-start(), calls=%async_computation.7 | async-start | bytes 1769472 | tf_op jit(solution)/shard_map/reduce_scatter | solution.py:127
  526.2 5.4 collective-permute-start.49
  527.5 5.6 collective-permute-start.50
  535.0 84.9 %reduce-scatter.12.cloned.1.call-start = ((), (), s32[]{:S(2)}) async-start(), calls=%async_computation.8 | async-start | bytes 1769472 | tf_op jit(solution)/shard_map/reduce_scatter | solution.py:127
  573.8 5.4 collective-permute-start.51
  575.3 5.2 collective-permute-start.52
  582.3 85.0 %reduce-scatter.14.cloned.1.call-start = ((), (), s32[]{:S(2)}) async-start(), calls=%async_computation.9 | async-start | bytes 1769472 | tf_op jit(solution)/shard_map/reduce_scatter | solution.py:127
  621.1 5.7 collective-permute-start.53
  622.5 5.2 collective-permute-start.54
  629.6 287.7 %all-reduce.8.cloned.1.call-start = ((), (), s32[]{:S(2)}) async-start(), calls=%async_computation.10 | async-start | bytes 21569536
  (36 other events, 733.4 us)
Sparse Core Ops, SparseCore 0:
  438.7 35.8 reduce-scatter.5
  485.4 39.6 reduce-scatter.7
  535.1 37.5 reduce-scatter.9
  582.4 37.4 reduce-scatter.11
  629.7 37.5 reduce-scatter.13
  672.4 244.7 all-reduce.7
